TPU v7x, 512 devices: a whole 4x4x16 slice. The times are simulated.
512 devices in a mesh: seq: 32 (over y_lo, z), head: 16 (over x, y_hi, core).
Axes of the slice: x: 4, y: 4 (y_hi: 2, y_lo: 2; y = y_hi * 2 + y_lo), z: 16, core: 2. Of those that a mesh axis runs over, the one named last changes fastest.
Arguments:
- queries: bfloat16 [65536, 2048], P(('seq', 'head')), may hold values from -27 to 27
- key_vectors: bfloat16 [65536, 2048], P(('seq', 'head')), may hold values from -6 to 6
- value_vectors: bfloat16 [65536, 2048], P(('seq', 'head')), may hold values from -6 to 6
- grad_output: bfloat16 [65536, 2048], P(('seq', 'head')), may hold values from -6 to 6
Outputs:
- grad_queries: bfloat16 [65536, 2048], P(('seq', 'head'))
- grad_keys: bfloat16 [65536, 2048], P(('seq', 'head'))
- grad_values: bfloat16 [65536, 2048], P(('seq', 'head'))
All inputs are finite; a program needn't handle non-finite values.
Results may differ from a plain program's by a relative error of at most 0.009.
Values may be sent and summed in bfloat16 or wider, within the bound.
A program may use at most 64 MiB of HBM per device.

v0:
```python
import jax
import jax.numpy as jnp
from jax import lax
from jax.sharding import PartitionSpec as P

HEADS = 16
HEAD_DIM = 128
WINDOW = 512


def from_behind(block, axis, distance):
    devices = range(lax.axis_size(axis))
    route = [(i - distance, i) for i in devices if i - distance in devices]
    return lax.ppermute(block, axis, route)


def scores_of(query_rows, key_rows, allowed):
    factor = HEAD_DIM ** (-0.5)
    scores = (
        jnp.einsum("rhe,che->hrc", query_rows, key_rows, preferred_element_type=jnp.float32)
        * factor
    )
    return jnp.where(allowed[None], scores, -1e30)


def stats_of(scores, value_rows, grad_rows):
    row_max = jnp.max(scores, axis=-1)
    log_total = row_max + jnp.log(jnp.sum(jnp.exp(scores - row_max[..., None]), axis=-1))
    probs_low = jnp.exp(scores - log_total[..., None]).astype(jnp.bfloat16)
    attn_out = jnp.einsum("hrc,che->hre", probs_low, value_rows, preferred_element_type=jnp.float32)
    row_dots = jnp.sum(jnp.transpose(grad_rows, (1, 0, 2)).astype(jnp.float32) * attn_out, axis=-1)
    return (log_total, row_dots)


def grads_of(scores, log_total, row_dots, query_rows, key_rows, value_rows, grad_rows):
    factor = HEAD_DIM ** (-0.5)
    attn_probs = jnp.exp(scores - log_total[..., None])
    probs_low = attn_probs.astype(jnp.bfloat16)
    grad_probs = jnp.einsum(
        "rhe,che->hrc", grad_rows, value_rows, preferred_element_type=jnp.float32
    )
    grad_scores = (attn_probs * (grad_probs - row_dots[..., None])).astype(jnp.bfloat16)
    grad_query = (
        jnp.einsum("hrc,che->rhe", grad_scores, key_rows, preferred_element_type=jnp.float32)
        * factor
    )
    grad_key = (
        jnp.einsum("hrc,rhe->che", grad_scores, query_rows, preferred_element_type=jnp.float32)
        * factor
    )
    grad_value = jnp.einsum(
        "hrc,rhe->che", probs_low, grad_rows, preferred_element_type=jnp.float32
    )
    return (grad_query, grad_key, grad_value)


def regrouped(queries, key_vectors, value_vectors, grad_output):
    head_group = HEADS // lax.axis_size("head")
    query_block, key_block, value_block, grad_block = (
        lax.all_to_all(queries, "head", split_axis=1, concat_axis=0, tiled=True),
        lax.all_to_all(key_vectors, "head", split_axis=1, concat_axis=0, tiled=True),
        lax.all_to_all(value_vectors, "head", split_axis=1, concat_axis=0, tiled=True),
        lax.all_to_all(grad_output, "head", split_axis=1, concat_axis=0, tiled=True),
    )
    block_rows = query_block.shape[0]
    shape = (block_rows, head_group, HEAD_DIM)
    query_block = query_block.reshape(shape)
    key_block = key_block.reshape(shape)
    value_block = value_block.reshape(shape)
    grad_block = grad_block.reshape(shape)
    blocks = block_rows // WINDOW
    key_tail = key_block[block_rows - WINDOW :]
    value_tail = value_block[block_rows - WINDOW :]
    key_halo, value_halo = from_behind((key_tail, value_tail), "seq", 1)
    key_ext = jnp.concatenate([key_halo, key_block], axis=0)
    value_ext = jnp.concatenate([value_halo, value_block], axis=0)
    first_shard = lax.axis_index("seq") == 0
    row_ids = jnp.arange(WINDOW, dtype=jnp.int32)[:, None]
    col_ids = jnp.arange(2 * WINDOW, dtype=jnp.int32)[None, :]
    band = (col_ids > row_ids) & (col_ids <= row_ids + WINDOW)

    def one_block(block_index):
        start = block_index * WINDOW
        query_rows = lax.dynamic_slice_in_dim(query_block, start, WINDOW, 0)
        grad_rows = lax.dynamic_slice_in_dim(grad_block, start, WINDOW, 0)
        key_rows = lax.dynamic_slice_in_dim(key_ext, start, 2 * WINDOW, 0)
        value_rows = lax.dynamic_slice_in_dim(value_ext, start, 2 * WINDOW, 0)
        allowed = band & ((col_ids >= WINDOW) | (block_index > 0) | jnp.logical_not(first_shard))
        scores = scores_of(query_rows, key_rows, allowed)
        log_total, row_dots = stats_of(scores, value_rows, grad_rows)
        grad_query, grad_key, grad_value = grads_of(
            scores, log_total, row_dots, query_rows, key_rows, value_rows, grad_rows
        )
        return (
            grad_query.astype(jnp.bfloat16),
            grad_key[:WINDOW],
            grad_key[WINDOW:],
            grad_value[:WINDOW],
            grad_value[WINDOW:],
            log_total,
            row_dots,
        )

    grad_query, key_front, key_back, value_front, value_back, log_total, row_dots = lax.map(
        one_block, jnp.arange(blocks, dtype=jnp.int32)
    )
    grad_key = key_back + jnp.concatenate([key_front[1:], jnp.zeros_like(key_front[:1])], axis=0)
    grad_value = value_back + jnp.concatenate(
        [value_front[1:], jnp.zeros_like(value_front[:1])], axis=0
    )
    key_later, value_later = from_behind((key_front[0], value_front[0]), "seq", -1)
    grad_key = grad_key.at[blocks - 1].add(key_later)
    grad_value = grad_value.at[blocks - 1].add(value_later)
    width = head_group * HEAD_DIM
    return (
        lax.all_to_all(
            grad_query.reshape(block_rows, width), "head", split_axis=0, concat_axis=1, tiled=True
        ),
        lax.all_to_all(
            grad_key.reshape(block_rows, width).astype(jnp.bfloat16),
            "head",
            split_axis=0,
            concat_axis=1,
            tiled=True,
        ),
        lax.all_to_all(
            grad_value.reshape(block_rows, width).astype(jnp.bfloat16),
            "head",
            split_axis=0,
            concat_axis=1,
            tiled=True,
        ),
    )


def per_device(queries, key_vectors, value_vectors, grad_output):
    return regrouped(queries, key_vectors, value_vectors, grad_output)


def solution(mesh):
    placed = (
        P(("seq", "head"), None),
        P(("seq", "head"), None),
        P(("seq", "head"), None),
        P(("seq", "head"), None),
    )
    return jax.shard_map(
        per_device,
        mesh=mesh,
        in_specs=placed,
        out_specs=(P(("seq", "head"), None), P(("seq", "head"), None), P(("seq", "head"), None)),
        check_vma=False,
    )
```

profile of v0, /device:TPU:8, one launch (start us, length us, event | category | flops | bytes accessed | tf_op | source)
XLA Modules:
  0.0 188.5 jit_solution(13152322102752312929)
XLA Ops:
  0.7 2.1 %copy.66 = bf16[128,2048]{0,1:T(8,128)(2,1)} copy(bf16[128,2048]{1,0:T(8,128)(2,1)} %param.10) | data formatting | bytes 1048576 | tf_op args[0]
  2.8 6.1 %all-to-all-start.1 = ((bf16[128,16,128]{0,2,1:T(8,128)(2,1)}), bf16[128,16,128]{0,2,1:T(8,128)(2,1)S(1)}, u32[]{:S(2)}, u32[]{:S(2)}) async-start(bf16[128,16,128]{0,2,1:T(8,128)(2,1)} %bitcast.4), calls=%async_computation.1 | async-start | bytes 1048576 | tf_op jit(solution)/shard_map/all_to_all | solution.py:60
  8.9 1.0 copy.63
  9.9 11.3 %all-to-all-done.1 = bf16[128,16,128]{0,2,1:T(8,128)(2,1)S(1)} async-done(((bf16[128,16,128]{0,2,1:T(8,128)(2,1)}), bf16[128,16,128]{0,2,1:T(8,128)(2,1)S(1)}, u32[]{:S(2)}, u32[]{:S(2)}) %all-to-all-start.1) | async-done | bytes 524320 | tf_op jit(solution)/shard_map/all_to_all | solution.py:60
  21.3 3.6 %all-to-all-start = ((bf16[128,16,128]{0,2,1:T(8,128)(2,1)}), bf16[128,16,128]{0,2,1:T(8,128)(2,1)S(1)}, u32[]{:S(2)}, u32[]{:S(2)}) async-start(bf16[128,16,128]{0,2,1:T(8,128)(2,1)} %bitcast), calls=%async_computation | async-start | bytes 1048576 | tf_op jit(solution)/shard_map/all_to_all | solution.py:61
  24.8 1.0 copy.70
  25.8 11.3 %all-to-all-done = bf16[128,16,128]{0,2,1:T(8,128)(2,1)S(1)} async-done(((bf16[128,16,128]{0,2,1:T(8,128)(2,1)}), bf16[128,16,128]{0,2,1:T(8,128)(2,1)S(1)}, u32[]{:S(2)}, u32[]{:S(2)}) %all-to-all-start) | async-done | bytes 524320 | tf_op jit(solution)/shard_map/all_to_all | solution.py:61
  37.1 3.6 %all-to-all-start.3 = ((bf16[128,16,128]{0,2,1:T(8,128)(2,1)}), bf16[128,16,128]{0,2,1:T(8,128)(2,1)S(1)}, u32[]{:S(2)}, u32[]{:S(2)}) async-start(bf16[128,16,128]{0,2,1:T(8,128)(2,1)} %bitcast.10), calls=%async_computation.3 | async-start | bytes 1048576 | tf_op jit(solution)/shard_map/all_to_all | solution.py:62
  40.7 1.0 copy.68
  41.7 11.3 %all-to-all-done.3 = bf16[128,16,128]{0,2,1:T(8,128)(2,1)S(1)} async-done(((bf16[128,16,128]{0,2,1:T(8,128)(2,1)}), bf16[128,16,128]{0,2,1:T(8,128)(2,1)S(1)}, u32[]{:S(2)}, u32[]{:S(2)}) %all-to-all-start.3) | async-done | bytes 524320 | tf_op jit(solution)/shard_map/all_to_all | solution.py:62
  53.0 3.6 %all-to-all-start.2 = ((bf16[128,16,128]{0,2,1:T(8,128)(2,1)}), bf16[128,16,128]{0,2,1:T(8,128)(2,1)S(1)}, u32[]{:S(2)}, u32[]{:S(2)}) async-start(bf16[128,16,128]{0,2,1:T(8,128)(2,1)} %bitcast.7), calls=%async_computation.2 | async-start | bytes 1048576 | tf_op jit(solution)/shard_map/all_to_all | solution.py:63
  56.8 3.8 %collective-permute-start = (bf16[512,1,128]{2,0,1:T(8,128)(2,1)S(1)}, bf16[512,1,128]{2,0,1:T(8,128)(2,1)S(1)}, u32[]{:S(2)}, u32[]{:S(2)}) collective-permute-start(bf16[512,1,128]{2,0,1:T(8,128)(2,1)S(1)} %bitcast.140), channel_id=1, source_target_pairs={{0,16},{16,32},{32,48},{48,64},{64,80},{80,96},{96,112},{112,128},... | collective-permute-start | bytes 393224 | tf_op jit(solution)/shard_map/ppermute | solution.py:14
  61.2 1.0 copy.67
  62.4 3.8 %collective-permute-start.1 = (bf16[512,1,128]{2,0,1:T(8,128)(2,1)S(1)}, bf16[512,1,128]{2,0,1:T(8,128)(2,1)S(1)}, u32[]{:S(2)}, u32[]{:S(2)}) collective-permute-start(bf16[512,1,128]{2,0,1:T(8,128)(2,1)S(1)} %bitcast.141), channel_id=1, source_target_pairs={{0,16},{16,32},{32,48},{48,64},{64,80},{80,96},{96,112},{112,128},... | collective-permute-start | bytes 393224 | tf_op jit(solution)/shard_map/ppermute | solution.py:14
  66.2 2.7 %all-to-all-done.2 = bf16[128,16,128]{0,2,1:T(8,128)(2,1)S(1)} async-done(((bf16[128,16,128]{0,2,1:T(8,128)(2,1)}), bf16[128,16,128]{0,2,1:T(8,128)(2,1)S(1)}, u32[]{:S(2)}, u32[]{:S(2)}) %all-to-all-start.2) | async-done | bytes 524320 | tf_op jit(solution)/shard_map/all_to_all | solution.py:63
  68.9 1.0 copy.69
  69.9 3.0 %collective-permute-done = bf16[512,1,128]{2,0,1:T(8,128)(2,1)S(1)} collective-permute-done((bf16[512,1,128]{2,0,1:T(8,128)(2,1)S(1)}, bf16[512,1,128]{2,0,1:T(8,128)(2,1)S(1)}, u32[]{:S(2)}, u32[]{:S(2)}) %collective-permute-start) | collective-permute-done | bytes 131104 | tf_op jit(solution)/shard_map/ppermute | solution.py:14
  72.9 3.7 %collective-permute-done.1 = bf16[512,1,128]{2,0,1:T(8,128)(2,1)S(1)} collective-permute-done((bf16[512,1,128]{2,0,1:T(8,128)(2,1)S(1)}, bf16[512,1,128]{2,0,1:T(8,128)(2,1)S(1)}, u32[]{:S(2)}, u32[]{:S(2)}) %collective-permute-start.1) | collective-permute-done | bytes 131104 | tf_op jit(solution)/shard_map/ppermute | solution.py:14
  76.7 46.0 %while.23 = (s32[]{:T(128)}, bf16[4,512,1,128]{3,1,0,2:T(8,128)(2,1)}, f32[4,512,1,128]{1,3,2,0:T(8,128)}, f32[4,512,1,128]{3,1,0,2:T(8,128)}, f32[4,512,1,128]{...) while((s32[]{:T(128)}, ...), condition=%wide.region_4.5_spmd.clone, body=%wide.region_0.4_spmd.clone.sunk | while | flops 814680064 | bytes 21784892 | solution.py:104
  78.7 0.9 constant_dynamic-slice_fusion.2
  79.8 1.7 fusion.64
  84.1 1.2 fusion.67
  90.2 0.9 constant_dynamic-slice_fusion.2
  91.3 1.7 fusion.64
  95.6 1.2 fusion.67
  101.7 0.9 constant_dynamic-slice_fusion.2
  102.7 1.7 fusion.64
  107.1 1.2 fusion.67
  113.2 0.9 constant_dynamic-slice_fusion.2
  114.2 1.7 fusion.64
  118.6 1.2 fusion.67
  122.7 2.7 %copy.78 = f32[4,512,1,128]{3,1,2,0:T(8,128)} copy(f32[4,512,1,128]{1,3,2,0:T(8,128)} %get-tuple-element.193) | data formatting | bytes 2097152 | tf_op jit(solution)/shard_map/while | solution.py:104
  125.7 1.3 copy.82
  127.4 6.4 %all-to-all-start.4 = ((bf16[16,128,128]{2,1,0:T(8,128)(2,1)}), bf16[16,128,128]{2,1,0:T(8,128)(2,1)}, u32[]{:S(2)}, u32[]{:S(2)}) async-start(bf16[16,128,128]{2,1,0:T(8,128)(2,1)} %bitcast.139), calls=%async_computation.4 | async-start | bytes 1048576 | tf_op jit(solution)/shard_map/all_to_all | solution.py:116
  133.8 1.1 slice_bitcast_fusion.5
  135.0 4.4 %collective-permute-start.2 = (f32[512,1,128]{2,0,1:T(8,128)S(1)}, f32[512,1,128]{2,0,1:T(8,128)S(1)}, u32[]{:S(2)}, u32[]{:S(2)}) collective-permute-start(f32[512,1,128]{2,0,1:T(8,128)S(1)} %slice_bitcast_fusion.5), channel_id=1, source_target_pairs={{16,0},{32,16},{48,32},{64,48},{80,64},{96,80},{112,96},{128,112},... | collective-permute-start | bytes 786440 | tf_op jit(solution)/shard_map/ppermute | solution.py:14
  139.4 1.0 slice_bitcast_fusion.4
  140.4 3.6 %collective-permute-start.3 = (f32[512,1,128]{2,0,1:T(8,128)S(1)}, f32[512,1,128]{2,0,1:T(8,128)S(1)}, u32[]{:S(2)}, u32[]{:S(2)}) collective-permute-start(f32[512,1,128]{2,0,1:T(8,128)S(1)} %slice_bitcast_fusion.4), channel_id=1, source_target_pairs={{16,0},{32,16},{48,32},{64,48},{80,64},{96,80},{112,96},{128,112},... | collective-permute-start | bytes 786440 | tf_op jit(solution)/shard_map/ppermute | solution.py:14
  144.3 8.1 %collective-permute-done.3 = f32[512,1,128]{2,0,1:T(8,128)S(1)} collective-permute-done((f32[512,1,128]{2,0,1:T(8,128)S(1)}, f32[512,1,128]{2,0,1:T(8,128)S(1)}, u32[]{:S(2)}, u32[]{:S(2)}) %collective-permute-start.3) | collective-permute-done | bytes 262176 | tf_op jit(solution)/shard_map/ppermute | solution.py:14
  152.4 0.9 convert_element_type.46
  153.3 5.7 %all-to-all-start.6 = ((bf16[16,128,128]{2,1,0:T(8,128)(2,1)}), bf16[16,128,128]{2,1,0:T(8,128)(2,1)S(1)}, u32[]{:S(2)}, u32[]{:S(2)}) async-start(bf16[16,128,128]{2,1,0:T(8,128)(2,1)} %bitcast.24), calls=%async_computation.6 | async-start | bytes 1048576 | tf_op jit(solution)/shard_map/all_to_all | solution.py:126
  160.0 11.4 %all-to-all-done.6 = bf16[16,128,128]{2,1,0:T(8,128)(2,1)S(1)} async-done(((bf16[16,128,128]{2,1,0:T(8,128)(2,1)}), bf16[16,128,128]{2,1,0:T(8,128)(2,1)S(1)}, u32[]{:S(2)}, u32[]{:S(2)}) %all-to-all-start.6) | async-done | bytes 524320 | tf_op jit(solution)/shard_map/all_to_all | solution.py:126
  171.4 3.6 %all-to-all-start.5 = ((bf16[16,128,128]{2,1,0:T(8,128)(2,1)}), bf16[16,128,128]{2,1,0:T(8,128)(2,1)S(1)}, u32[]{:S(2)}, u32[]{:S(2)}) async-start(bf16[16,128,128]{2,1,0:T(8,128)(2,1)} %bitcast.19), calls=%async_computation.5 | async-start | bytes 1048576 | tf_op jit(solution)/shard_map/all_to_all | solution.py:119
  175.0 1.3 copy.75
  176.3 1.0 copy.84
  177.6 1.0 copy.86
  178.6 8.7 %all-to-all-done.5 = bf16[16,128,128]{2,1,0:T(8,128)(2,1)S(1)} async-done(((bf16[16,128,128]{2,1,0:T(8,128)(2,1)}), bf16[16,128,128]{2,1,0:T(8,128)(2,1)S(1)}, u32[]{:S(2)}, u32[]{:S(2)}) %all-to-all-start.5) | async-done | bytes 524320 | tf_op jit(solution)/shard_map/all_to_all | solution.py:119
  187.5 1.0 copy.85
  (112 shorter events, 28.4 us)
Async XLA Ops:
  0.6 8.3 %copy-start.5 = (bf16[128,2048]{1,0:T(8,128)(2,1)S(1)}, bf16[128,2048]{1,0:T(8,128)(2,1)}, u32[]{:S(2)}) copy-start(bf16[128,2048]{1,0:T(8,128)(2,1)} %param.11) | copy-start | bytes 1572868
  0.6 24.2 %copy-start.6 = (bf16[128,2048]{1,0:T(8,128)(2,1)S(1)}, bf16[128,2048]{1,0:T(8,128)(2,1)}, u32[]{:S(2)}) copy-start(bf16[128,2048]{1,0:T(8,128)(2,1)} %param.12) | copy-start | bytes 1572868
  2.8 18.5 %all-to-all-start.1 = ((bf16[128,16,128]{0,2,1:T(8,128)(2,1)}), bf16[128,16,128]{0,2,1:T(8,128)(2,1)S(1)}, u32[]{:S(2)}, u32[]{:S(2)}) async-start(bf16[128,16,128]{0,2,1:T(8,128)(2,1)} %bitcast.4), calls=%async_computation.1 | async-start | bytes 1048576 | tf_op jit(solution)/shard_map/all_to_all | solution.py:60
  8.9 31.8 %copy-start.7 = (bf16[128,2048]{1,0:T(8,128)(2,1)S(1)}, bf16[128,2048]{1,0:T(8,128)(2,1)}, u32[]{:S(2)}) copy-start(bf16[128,2048]{1,0:T(8,128)(2,1)} %param.13) | copy-start | bytes 1572868
  21.3 15.9 %all-to-all-start = ((bf16[128,16,128]{0,2,1:T(8,128)(2,1)}), bf16[128,16,128]{0,2,1:T(8,128)(2,1)S(1)}, u32[]{:S(2)}, u32[]{:S(2)}) async-start(bf16[128,16,128]{0,2,1:T(8,128)(2,1)} %bitcast), calls=%async_computation | async-start | bytes 1048576 | tf_op jit(solution)/shard_map/all_to_all | solution.py:61
  37.1 15.9 %all-to-all-start.3 = ((bf16[128,16,128]{0,2,1:T(8,128)(2,1)}), bf16[128,16,128]{0,2,1:T(8,128)(2,1)S(1)}, u32[]{:S(2)}, u32[]{:S(2)}) async-start(bf16[128,16,128]{0,2,1:T(8,128)(2,1)} %bitcast.10), calls=%async_computation.3 | async-start | bytes 1048576 | tf_op jit(solution)/shard_map/all_to_all | solution.py:62
  53.0 15.9 %all-to-all-start.2 = ((bf16[128,16,128]{0,2,1:T(8,128)(2,1)}), bf16[128,16,128]{0,2,1:T(8,128)(2,1)S(1)}, u32[]{:S(2)}, u32[]{:S(2)}) async-start(bf16[128,16,128]{0,2,1:T(8,128)(2,1)} %bitcast.7), calls=%async_computation.2 | async-start | bytes 1048576 | tf_op jit(solution)/shard_map/all_to_all | solution.py:63
  56.8 16.1 %collective-permute-start = (bf16[512,1,128]{2,0,1:T(8,128)(2,1)S(1)}, bf16[512,1,128]{2,0,1:T(8,128)(2,1)S(1)}, u32[]{:S(2)}, u32[]{:S(2)}) collective-permute-start(bf16[512,1,128]{2,0,1:T(8,128)(2,1)S(1)} %bitcast.140), channel_id=1, source_target_pairs={{0,16},{16,32},{32,48},{48,64},{64,80},{80,96},{96,112},{112,128},... | collective-permute-start | bytes 393224 | tf_op jit(solution)/shard_map/ppermute | solution.py:14
  62.4 14.2 %collective-permute-start.1 = (bf16[512,1,128]{2,0,1:T(8,128)(2,1)S(1)}, bf16[512,1,128]{2,0,1:T(8,128)(2,1)S(1)}, u32[]{:S(2)}, u32[]{:S(2)}) collective-permute-start(bf16[512,1,128]{2,0,1:T(8,128)(2,1)S(1)} %bitcast.141), channel_id=1, source_target_pairs={{0,16},{16,32},{32,48},{48,64},{64,80},{80,96},{96,112},{112,128},... | collective-permute-start | bytes 393224 | tf_op jit(solution)/shard_map/ppermute | solution.py:14
  122.7 2.7 %copy-start.1 = (f32[4,512,1,128]{1,3,2,0:T(8,128)S(1)}, f32[4,512,1,128]{1,3,2,0:T(8,128)}, u32[]{:S(2)}) copy-start(f32[4,512,1,128]{1,3,2,0:T(8,128)} %get-tuple-element.193) | copy-start | bytes 3145732
  122.7 3.0 %copy-start = (f32[4,512,1,128]{1,3,2,0:T(8,128)S(1)}, f32[4,512,1,128]{1,3,2,0:T(8,128)}, u32[]{:S(2)}) copy-start(f32[4,512,1,128]{1,3,2,0:T(8,128)} %get-tuple-element.195) | copy-start | bytes 3145732
  125.7 9.3 %copy-start.2 = (f32[4,512,1,128]{3,1,0,2:T(8,128)}, f32[4,512,1,128]{3,1,0,2:T(8,128)S(1)}, u32[]{:S(2)}) copy-start(f32[4,512,1,128]{3,1,0,2:T(8,128)S(1)} %copy.76) | copy-start | bytes 3145732
  127.4 26.0 %all-to-all-start.4 = ((bf16[16,128,128]{2,1,0:T(8,128)(2,1)}), bf16[16,128,128]{2,1,0:T(8,128)(2,1)}, u32[]{:S(2)}, u32[]{:S(2)}) async-start(bf16[16,128,128]{2,1,0:T(8,128)(2,1)} %bitcast.139), calls=%async_computation.4 | async-start | bytes 1048576 | tf_op jit(solution)/shard_map/all_to_all | solution.py:116
  133.8 10.2 %copy-start.3 = (f32[4,512,1,128]{3,1,0,2:T(8,128)S(1)}, f32[4,512,1,128]{3,1,0,2:T(8,128)}, u32[]{:S(2)}) copy-start(f32[4,512,1,128]{3,1,0,2:T(8,128)} %get-tuple-element.194) | copy-start | bytes 3145732
  133.8 10.2 %copy-start.4 = (f32[4,512,1,128]{3,1,0,2:T(8,128)S(1)}, f32[4,512,1,128]{3,1,0,2:T(8,128)}, u32[]{:S(2)}) copy-start(f32[4,512,1,128]{3,1,0,2:T(8,128)} %get-tuple-element.192) | copy-start | bytes 3145732
  135.0 9.1 %slice-start = ((f32[4,512,1,128]{3,1,0,2:T(8,128)}), f32[3,512,1,128]{3,1,0,2:T(8,128)S(1)}, s32[]{:S(2)}) async-start(f32[4,512,1,128]{3,1,0,2:T(8,128)} %copy-done.2), calls=%async_computation.7 | async-start | bytes 1572864 | tf_op jit(solution)/shard_map/slice | solution.py:107
  135.0 24.1 %collective-permute-start.2 = (f32[512,1,128]{2,0,1:T(8,128)S(1)}, f32[512,1,128]{2,0,1:T(8,128)S(1)}, u32[]{:S(2)}, u32[]{:S(2)}) collective-permute-start(f32[512,1,128]{2,0,1:T(8,128)S(1)} %slice_bitcast_fusion.5), channel_id=1, source_target_pairs={{16,0},{32,16},{48,32},{64,48},{80,64},{96,80},{112,96},{128,112},... | collective-permute-start | bytes 786440 | tf_op jit(solution)/shard_map/ppermute | solution.py:14
  140.4 12.0 %collective-permute-start.3 = (f32[512,1,128]{2,0,1:T(8,128)S(1)}, f32[512,1,128]{2,0,1:T(8,128)S(1)}, u32[]{:S(2)}, u32[]{:S(2)}) collective-permute-start(f32[512,1,128]{2,0,1:T(8,128)S(1)} %slice_bitcast_fusion.4), channel_id=1, source_target_pairs={{16,0},{32,16},{48,32},{64,48},{80,64},{96,80},{112,96},{128,112},... | collective-permute-start | bytes 786440 | tf_op jit(solution)/shard_map/ppermute | solution.py:14
  153.3 18.1 %all-to-all-start.6 = ((bf16[16,128,128]{2,1,0:T(8,128)(2,1)}), bf16[16,128,128]{2,1,0:T(8,128)(2,1)S(1)}, u32[]{:S(2)}, u32[]{:S(2)}) async-start(bf16[16,128,128]{2,1,0:T(8,128)(2,1)} %bitcast.24), calls=%async_computation.6 | async-start | bytes 1048576 | tf_op jit(solution)/shard_map/all_to_all | solution.py:126
  171.4 15.9 %all-to-all-start.5 = ((bf16[16,128,128]{2,1,0:T(8,128)(2,1)}), bf16[16,128,128]{2,1,0:T(8,128)(2,1)S(1)}, u32[]{:S(2)}, u32[]{:S(2)}) async-start(bf16[16,128,128]{2,1,0:T(8,128)(2,1)} %bitcast.19), calls=%async_computation.5 | async-start | bytes 1048576 | tf_op jit(solution)/shard_map/all_to_all | solution.py:119
where the time goes:
time: 190 us; the launch traced here: 189 us
  waiting for transfers between devices  71.4 us (38%)
  starting transfers between devices  48.3 us (25%)
  local copies, waits for them, and re-layouts  37.4 us (20%)
  matrix products  20.3 us (11%)
  loops' own time  5.78 us (3%)
  other arithmetic  4.34 us (2%)
    ppermute x4, starting transfers between devices, from_behind(): return lax.ppermute(block, axis, route)  15.7 us
    ppermute x4, waiting for transfers between devices, from_behind(): return lax.ppermute(block, axis, route)  14.8 us
    all_to_all x1, waiting for transfers between devices, regrouped(): lax.all_to_all(grad_value.reshape(block_rows, width).astype(jnp.bfloat16)...  11.4 us
    all_to_all x1, waiting for transfers between devices, regrouped(): lax.all_to_all(queries, 'head', split_axis=1, concat_axis=0, tiled=True)  11.3 us
    all_to_all x1, waiting for transfers between devices, regrouped(): lax.all_to_all(key_vectors, 'head', split_axis=1, concat_axis=0, tiled=True)  11.3 us
    all_to_all x1, waiting for transfers between devices, regrouped(): lax.all_to_all(value_vectors, 'head', split_axis=1, concat_axis=0, tiled=...  11.3 us
    dynamic_update_slice x24, local copies, waits for them, and re-layouts, regrouped(): lax.map(one_block, jnp.arange(blocks, dtype=jnp.int32))  10.8 us
    all_to_all x1, waiting for transfers between devices, regrouped(): lax.all_to_all(grad_key.reshape(block_rows, width).astype(jnp.bfloat16),...  8.67 us
  transfers between devices with their start and end apart: 11, of which 9 were waited for; matrix products, arithmetic and copies ran while one was open for 7% of the time, Pallas kernels for 0%

commit v1 on v0

v1 whole, which is shorter than its diff:
```python
import functools

import jax
import jax.numpy as jnp
from jax import lax
from jax.experimental import pallas as pl
from jax.experimental.pallas import tpu as pltpu
from jax.sharding import PartitionSpec as P

HEAD_DIM = 128
CHUNK = 256
CHUNKS = 8
HALO = 2
ROWS = 128
SCALE = HEAD_DIM ** (-0.5)
LOG2E = 1.4426950408889634
NEG = -1e30
MESH = pl.DeviceIdType.MESH
K, V, Q, G, DQ, DK, DV = range(7)
NT = (((1,), (1,)), ((), ()))


def kernel(
    q_hbm, k_hbm, v_hbm, g_hbm,
    dq_hbm, dk_hbm, dv_hbm,
    kbuf, vbuf, qbuf, gbuf, kt, probs, dprobs,
    dk_acc, dv_acc, dq_out, dk_out, dv_out, part_k, part_v,
    send_sem, recv_sem, hs_sem, hr_sem,
):
    s = lax.axis_index("seq")
    me = lax.axis_index("head")
    blocks = lax.axis_size("seq")
    chip, core = me // 2, me % 2
    cx, cy = chip // 2, chip % 2
    first = s == 0
    last = s == blocks - 1

    def partner_chip(o):
        return ((cx + o // 2) % 4) * 2 + (cy + o) % 2

    others = [(o, d) for o in range(8) for d in range(2) if (o, d) != (0, 0)]

    def device(o, d):
        return partner_chip(o) * 2 + (core + d) % 2

    barrier = pltpu.get_barrier_semaphore()
    for o, d in others:
        pl.semaphore_signal(barrier, inc=1, device_id=(s, device(o, d)), device_id_type=MESH)

    @pl.when(jnp.logical_not(first))
    def _():
        pl.semaphore_signal(barrier, inc=1, device_id=(s - 1, me), device_id_type=MESH)

    @pl.when(jnp.logical_not(last))
    def _():
        pl.semaphore_signal(barrier, inc=1, device_id=(s + 1, me), device_id_type=MESH)

    inputs = {K: (k_hbm, kbuf, HALO * CHUNK), V: (v_hbm, vbuf, HALO * CHUNK), Q: (q_hbm, qbuf, 0), G: (g_hbm, gbuf, 0)}

    def rows(start, size):
        return pl.ds(pl.multiple_of(start, ROWS), size)

    def local_in(a):
        src, dst, base = inputs[a]
        return pltpu.make_async_copy(
            src.at[:, rows(me * ROWS, HEAD_DIM)], dst.at[rows(base + me * ROWS, ROWS)], recv_sem.at[a, me]
        )

    def remote_in(a, to, source):
        src, dst, base = inputs[a]
        return pltpu.make_async_remote_copy(
            src.at[:, rows(to * HEAD_DIM, HEAD_DIM)],
            dst.at[rows(base + source * ROWS, ROWS)],
            send_sem.at[a, to],
            recv_sem.at[a, source],
            device_id=(s, to),
            device_id_type=MESH,
        )

    for a in (K, V, Q, G):
        local_in(a).start()

    zero = jnp.zeros((HALO * CHUNK, HEAD_DIM), jnp.bfloat16)

    @pl.when(first)
    def _():
        kbuf[: HALO * CHUNK] = zero
        vbuf[: HALO * CHUNK] = zero

    dk_acc[...] = jnp.zeros_like(dk_acc)
    dv_acc[...] = jnp.zeros_like(dv_acc)

    count = 15 + jnp.where(first, 0, 1) + jnp.where(last, 0, 1)
    pl.semaphore_wait(barrier, count)

    for a in (K, V, Q, G):
        for o, d in others:
            remote_in(a, device(o, d), me).start()

    def wait_in(a, o):
        for d in range(2):
            if isinstance(o, int):
                if (o, d) == (0, 0):
                    local_in(a).wait()
                else:
                    remote_in(a, me, device(o, d)).wait_recv()
            else:
                remote_in(a, me, device(o, d)).wait_recv()

    def halo(i, buf):
        return pltpu.make_async_remote_copy(
            buf.at[pl.ds(CHUNKS * CHUNK, HALO * CHUNK)],
            buf.at[pl.ds(0, HALO * CHUNK)],
            hs_sem.at[i],
            hr_sem.at[i],
            device_id=(s + 1, me),
            device_id_type=MESH,
        )

    for i, (a, buf) in enumerate(((K, kbuf), (V, vbuf))):
        for o in range(8):
            wait_in(a, o)

        @pl.when(jnp.logical_not(last))
        def _():
            halo(i, buf).start()

        if a == K:

            @pl.loop(HALO, HALO + CHUNKS)
            def _(b):
                kt[b] = kbuf[rows(b * CHUNK, CHUNK), :].T

    @pl.when(jnp.logical_not(first))
    def _():
        halo(0, kbuf).wait_recv()

    for b in range(HALO):
        kt[b] = kbuf[b * CHUNK : (b + 1) * CHUNK, :].T

    key_ids = lax.broadcasted_iota(jnp.int32, (CHUNK, CHUNK), 0)
    query_ids = lax.broadcasted_iota(jnp.int32, (CHUNK, CHUNK), 1)

    def softmax(c):
        queries = qbuf[rows(c * CHUNK, CHUNK), :]
        top = None
        for b in range(3):
            scores = lax.dot_general(
                kbuf[rows((c + b) * CHUNK, CHUNK), :], queries, NT, preferred_element_type=jnp.float32
            )
            if b == 0:
                scores = jnp.where(key_ids > query_ids, scores, NEG)
            if b == 2:
                scores = jnp.where(key_ids <= query_ids, scores, NEG)
            if b < 2:
                scores = scores + jnp.where(first & (c + b < HALO), NEG, 0.0)
            probs[c, b] = scores
            best = jnp.max(scores, axis=0, keepdims=True)
            top = best if top is None else jnp.maximum(top, best)
        total = None
        for b in range(3):
            e = jnp.exp2((probs[c, b] - top) * (SCALE * LOG2E))
            probs[c, b] = e
            part = jnp.sum(e, axis=0, keepdims=True)
            total = part if total is None else total + part
        inverse = 1.0 / total
        for b in range(3):
            probs[c, b] = probs[c, b] * inverse

    for o in range(8):
        wait_in(Q, o)

    @pl.loop(0, CHUNKS)
    def _(c):
        softmax(c)

    @pl.when(jnp.logical_not(first))
    def _():
        halo(1, vbuf).wait_recv()

    def gradients(c):
        queries = qbuf[rows(c * CHUNK, CHUNK), :]
        grads = gbuf[rows(c * CHUNK, CHUNK), :]
        dots = None
        for b in range(3):
            window = rows((c + b) * CHUNK, CHUNK)
            p = probs[c, b]
            dv_acc[window, :] += jnp.dot(p.astype(jnp.bfloat16), grads, preferred_element_type=jnp.float32)
            dp = lax.dot_general(vbuf[window, :], grads, NT, preferred_element_type=jnp.float32)
            dprobs[b] = dp
            part = jnp.sum(p * dp, axis=0, keepdims=True)
            dots = part if dots is None else dots + part
        dq = None
        for b in range(3):
            window = rows((c + b) * CHUNK, CHUNK)
            ds = (probs[c, b] * (dprobs[b] - dots)).astype(jnp.bfloat16)
            dk_acc[window, :] += jnp.dot(ds, queries, preferred_element_type=jnp.float32)
            part = jnp.dot(kt[c + b], ds, preferred_element_type=jnp.float32)
            dq = part if dq is None else dq + part
        dq_out[rows(c * CHUNK, CHUNK), :] = (dq * SCALE).T.astype(jnp.bfloat16)

    outputs = {DQ: (dq_out, dq_hbm), DK: (dk_out, dk_hbm), DV: (dv_out, dv_hbm)}

    def local_out(a):
        src, dst = outputs[a]
        return pltpu.make_async_copy(
            src.at[rows(me * ROWS, ROWS)], dst.at[:, rows(me * HEAD_DIM, HEAD_DIM)], recv_sem.at[a, me]
        )

    def remote_out(a, to, source):
        src, dst = outputs[a]
        return pltpu.make_async_remote_copy(
            src.at[rows(to * ROWS, ROWS)],
            dst.at[:, rows(source * HEAD_DIM, HEAD_DIM)],
            send_sem.at[a, to],
            recv_sem.at[a, source],
            device_id=(s, to),
            device_id_type=MESH,
        )

    def send_out(a, c):
        for d in range(2):
            to = c * 2 + d

            @pl.when(to == me)
            def _():
                local_out(a).start()

            @pl.when(to != me)
            def _():
                remote_out(a, to, me).start()

    for o in range(8):
        wait_in(G, o)

    @pl.loop(0, CHUNKS)
    def _(o):
        c = partner_chip(o)
        gradients(c)
        send_out(DQ, c)

    def back(i, src, dst):
        return pltpu.make_async_remote_copy(
            src.at[pl.ds(CHUNKS * CHUNK, HALO * CHUNK)],
            dst,
            hs_sem.at[2 + i],
            hr_sem.at[2 + i],
            device_id=(s - 1, me),
            device_id_type=MESH,
        )

    tail = pl.ds(CHUNKS * CHUNK, HALO * CHUNK)

    @pl.when(jnp.logical_not(first))
    def _():
        dk_out[tail, :] = (dk_acc[: HALO * CHUNK] * SCALE).astype(jnp.bfloat16)
        dv_out[tail, :] = dv_acc[: HALO * CHUNK].astype(jnp.bfloat16)
        back(0, dk_out, part_k).start()
        back(1, dv_out, part_v).start()

    @pl.loop(0, 6)
    def _(i):
        c = (chip + i) % 6
        src = rows((c + HALO) * CHUNK, CHUNK)
        dst = rows(c * CHUNK, CHUNK)
        dv_out[dst, :] = dv_acc[src, :].astype(jnp.bfloat16)
        send_out(DV, c)
        dk_out[dst, :] = (dk_acc[src, :] * SCALE).astype(jnp.bfloat16)
        send_out(DK, c)

    @pl.when(last)
    def _():
        part_k[...] = zero
        part_v[...] = zero

    @pl.when(jnp.logical_not(last))
    def _():
        back(0, dk_out, part_k).wait_recv()
        back(1, dv_out, part_v).wait_recv()

    @pl.loop(0, HALO)
    def _(i):
        p = (chip + i) % HALO
        c = 6 + p
        src = rows((c + HALO) * CHUNK, CHUNK)
        dst = rows(c * CHUNK, CHUNK)
        term = rows(p * CHUNK, CHUNK)
        dv_out[dst, :] = (dv_acc[src, :] + part_v[term, :].astype(jnp.float32)).astype(jnp.bfloat16)
        send_out(DV, c)
        dk_out[dst, :] = (dk_acc[src, :] * SCALE + part_k[term, :].astype(jnp.float32)).astype(jnp.bfloat16)
        send_out(DK, c)

    for a in (K, V, Q, G):
        for o, d in others:
            remote_in(a, device(o, d), me).wait_send()

    @pl.when(jnp.logical_not(last))
    def _():
        halo(0, kbuf).wait_send()
        halo(1, vbuf).wait_send()

    @pl.when(jnp.logical_not(first))
    def _():
        back(0, dk_out, part_k).wait_send()
        back(1, dv_out, part_v).wait_send()

    for a in (DQ, DK, DV):
        local_out(a).wait()
        for o, d in others:
            remote_out(a, device(o, d), me).wait_send()
            remote_out(a, me, device(o, d)).wait_recv()


def per_device(queries, key_vectors, value_vectors, grad_output):
    tokens, width = queries.shape
    bf16, f32 = jnp.bfloat16, jnp.float32
    own, wide = CHUNKS * CHUNK, (CHUNKS + HALO) * CHUNK
    out = jax.ShapeDtypeStruct((tokens, width), bf16)
    anywhere = pl.BlockSpec(memory_space=pl.ANY)
    return pl.pallas_call(
        kernel,
        out_shape=(out, out, out),
        in_specs=[anywhere] * 4,
        out_specs=(anywhere,) * 3,
        scratch_shapes=[
            pltpu.VMEM((wide, HEAD_DIM), bf16),
            pltpu.VMEM((wide, HEAD_DIM), bf16),
            pltpu.VMEM((own, HEAD_DIM), bf16),
            pltpu.VMEM((own, HEAD_DIM), bf16),
            pltpu.VMEM((CHUNKS + HALO, HEAD_DIM, CHUNK), bf16),
            pltpu.VMEM((CHUNKS, 3, CHUNK, CHUNK), f32),
            pltpu.VMEM((3, CHUNK, CHUNK), f32),
            pltpu.VMEM((wide, HEAD_DIM), f32),
            pltpu.VMEM((wide, HEAD_DIM), f32),
            pltpu.VMEM((own, HEAD_DIM), bf16),
            pltpu.VMEM((wide, HEAD_DIM), bf16),
            pltpu.VMEM((wide, HEAD_DIM), bf16),
            pltpu.VMEM((HALO * CHUNK, HEAD_DIM), bf16),
            pltpu.VMEM((HALO * CHUNK, HEAD_DIM), bf16),
            pltpu.SemaphoreType.DMA((7, 16)),
            pltpu.SemaphoreType.DMA((7, 16)),
            pltpu.SemaphoreType.DMA((4,)),
            pltpu.SemaphoreType.DMA((4,)),
        ],
        compiler_params=pltpu.CompilerParams(
            collective_id=0, has_side_effects=True, vmem_limit_bytes=48 * 1024 * 1024
        ),
        name="window_attention_backward",
    )(queries, key_vectors, value_vectors, grad_output)


def solution(mesh):
    placed = P(("seq", "head"), None)
    return jax.shard_map(
        per_device,
        mesh=mesh,
        in_specs=(placed,) * 4,
        out_specs=(placed,) * 3,
        check_vma=False,
    )
```

time: 190 us -> 73.4 us (0.39)
  the two profiles are of different devices: /device:TPU:8 before, /device:TPU:7 now
where the time goes in v1:
time: 73.4 us; the launch traced here: 73.1 us
  Pallas kernels  65.9 us (90%)
  local copies, waits for them, and re-layouts  6.54 us (9%)
    pallas_call x1, Pallas kernels, per_device(): pl.pallas_call(kernel, out_shape=(out, out, out), in_specs=[anywhere] * 4...  65.9 us
    unnamed x11, local copies, waits for them, and re-layouts  6.54 us

profile of v1, /device:TPU:7, one launch (start us, length us, event | category | flops | bytes accessed | tf_op | source)
XLA Modules:
  0.0 73.1 jit_solution(11327980345291209657)
XLA Ops:
  0.6 0.0 copy-start
  0.6 1.0 %copy-done = bf16[128,2048]{1,0:T(8,128)(2,1)S(1)} copy-done((bf16[128,2048]{1,0:T(8,128)(2,1)S(1)}, bf16[128,2048]{1,0:T(8,128)(2,1)}, u32[]{:S(2)}) %copy-start) | copy-done | bytes 524312
  1.7 0.0 copy-start.1
  1.7 1.0 %copy-done.1 = bf16[128,2048]{1,0:T(8,128)(2,1)S(1)} copy-done((bf16[128,2048]{1,0:T(8,128)(2,1)S(1)}, bf16[128,2048]{1,0:T(8,128)(2,1)}, u32[]{:S(2)}) %copy-start.1) | copy-done | bytes 524312
  2.7 0.0 copy-start.2
  2.7 1.0 %copy-done.2 = bf16[128,2048]{1,0:T(8,128)(2,1)S(1)} copy-done((bf16[128,2048]{1,0:T(8,128)(2,1)S(1)}, bf16[128,2048]{1,0:T(8,128)(2,1)}, u32[]{:S(2)}) %copy-start.2) | copy-done | bytes 524312
  3.8 0.0 copy-start.3
  3.8 1.0 %copy-done.3 = bf16[128,2048]{1,0:T(8,128)(2,1)S(1)} copy-done((bf16[128,2048]{1,0:T(8,128)(2,1)S(1)}, bf16[128,2048]{1,0:T(8,128)(2,1)}, u32[]{:S(2)}) %copy-start.3) | copy-done | bytes 524312
  4.8 65.9 %window_attention_backward.1 = (bf16[128,2048]{1,0:T(8,128)(2,1)S(1)}, bf16[128,2048]{1,0:T(8,128)(2,1)S(1)}, bf16[128,2048]{1,0:T(8,128)(2,1)S(1)}) custom-call(bf16[128,2048]{1,0:T(8,128)(2,1)S(1)} %copy-done, bf16[128,2048]{1,0:T(8,128)(2,1)S(1)} %copy-done.1, bf16[128,2048]{1,0:T(8,128)(2,1)S(1)} %copy-done.2, bf16[128,2048]{1,0:T(8,128)(2,1)S(1)} %copy-done.3), custom_call_target="tpu_custom_call" | custom-call | tf_op jit(solution)/shard_map/window_attention_backward/pallas_call | solution.py:320
  70.7 0.8 %copy.10 = bf16[128,2048]{1,0:T(8,128)(2,1)} copy(bf16[128,2048]{1,0:T(8,128)(2,1)S(1)} %get-tuple-element.6) | data formatting | bytes 1048576
  71.5 0.8 %copy.11 = bf16[128,2048]{1,0:T(8,128)(2,1)} copy(bf16[128,2048]{1,0:T(8,128)(2,1)S(1)} %get-tuple-element.7) | data formatting | bytes 1048576
  72.3 0.8 %copy.12 = bf16[128,2048]{1,0:T(8,128)(2,1)} copy(bf16[128,2048]{1,0:T(8,128)(2,1)S(1)} %get-tuple-element.8) | data formatting | bytes 1048576
Async XLA Ops:
  0.6 1.0 %copy-start = (bf16[128,2048]{1,0:T(8,128)(2,1)S(1)}, bf16[128,2048]{1,0:T(8,128)(2,1)}, u32[]{:S(2)}) copy-start(bf16[128,2048]{1,0:T(8,128)(2,1)} %q_hbm.1) | copy-start | bytes 1572868
  1.7 1.0 %copy-start.1 = (bf16[128,2048]{1,0:T(8,128)(2,1)S(1)}, bf16[128,2048]{1,0:T(8,128)(2,1)}, u32[]{:S(2)}) copy-start(bf16[128,2048]{1,0:T(8,128)(2,1)} %k_hbm.1) | copy-start | bytes 1572868
  2.7 1.0 %copy-start.2 = (bf16[128,2048]{1,0:T(8,128)(2,1)S(1)}, bf16[128,2048]{1,0:T(8,128)(2,1)}, u32[]{:S(2)}) copy-start(bf16[128,2048]{1,0:T(8,128)(2,1)} %v_hbm.1) | copy-start | bytes 1572868
  3.8 1.0 %copy-start.3 = (bf16[128,2048]{1,0:T(8,128)(2,1)S(1)}, bf16[128,2048]{1,0:T(8,128)(2,1)}, u32[]{:S(2)}) copy-start(bf16[128,2048]{1,0:T(8,128)(2,1)} %g_hbm.1) | copy-start | bytes 1572868

commit v2 on v1

--- a/solution.py
+++ b/solution.py
@@ -11,6 +11,7 @@
 CHUNK = 256
 CHUNKS = 8
 HALO = 2
+RING = 16
 ROWS = 128
 SCALE = HEAD_DIM ** (-0.5)
 LOG2E = 1.4426950408889634
@@ -25,7 +26,7 @@
     dq_hbm, dk_hbm, dv_hbm,
     kbuf, vbuf, qbuf, gbuf, kt, probs, dprobs,
     dk_acc, dv_acc, dq_out, dk_out, dv_out, part_k, part_v,
-    send_sem, recv_sem, hs_sem, hr_sem,
+    send_sem, recv_sem, hs_sem, hr_sem, late_sem, next_sem, prev_sem,
 ):
     s = lax.axis_index("seq")
     me = lax.axis_index("head")
@@ -43,17 +44,29 @@
     def device(o, d):
         return partner_chip(o) * 2 + (core + d) % 2
 
+    late = first & (me == 0)
+    with_late = first & (me != 0)
+    starts = s % RING == 0
+    ends = (s + 1) % RING == 0
+    has_prev, has_next = jnp.logical_not(first), jnp.logical_not(last)
+
+    def signal(sem, block, head):
+        pl.semaphore_signal(sem, inc=1, device_id=(block, head), device_id_type=MESH)
+
     barrier = pltpu.get_barrier_semaphore()
-    for o, d in others:
-        pl.semaphore_signal(barrier, inc=1, device_id=(s, device(o, d)), device_id_type=MESH)
-
-    @pl.when(jnp.logical_not(first))
-    def _():
-        pl.semaphore_signal(barrier, inc=1, device_id=(s - 1, me), device_id_type=MESH)
-
-    @pl.when(jnp.logical_not(last))
-    def _():
-        pl.semaphore_signal(barrier, inc=1, device_id=(s + 1, me), device_id_type=MESH)
+
+    @pl.when(jnp.logical_not(late))
+    def _():
+        for o, d in others:
+            signal(barrier, s, device(o, d))
+
+    @pl.when(has_next & jnp.logical_not(ends))
+    def _():
+        signal(barrier, s + 1, me)
+
+    @pl.when(has_prev & starts)
+    def _():
+        signal(barrier, s - 1, me)
 
     inputs = {K: (k_hbm, kbuf, HALO * CHUNK), V: (v_hbm, vbuf, HALO * CHUNK), Q: (q_hbm, qbuf, 0), G: (g_hbm, gbuf, 0)}
 
@@ -90,22 +103,44 @@
     dk_acc[...] = jnp.zeros_like(dk_acc)
     dv_acc[...] = jnp.zeros_like(dv_acc)
 
-    count = 15 + jnp.where(first, 0, 1) + jnp.where(last, 0, 1)
+    count = 15 - with_late.astype(jnp.int32) + jnp.logical_not(starts).astype(jnp.int32)
+    count = count + (has_next & ends).astype(jnp.int32)
     pl.semaphore_wait(barrier, count)
+
+    @pl.when(late)
+    def _():
+        for o, d in others:
+            signal(late_sem, s, device(o, d))
+
+    @pl.when(has_prev & jnp.logical_not(starts))
+    def _():
+        signal(next_sem, s - 1, me)
+
+    @pl.when(has_next & ends)
+    def _():
+        signal(prev_sem, s + 1, me)
 
     for a in (K, V, Q, G):
         for o, d in others:
-            remote_in(a, device(o, d), me).start()
-
-    def wait_in(a, o):
+            to = device(o, d)
+
+            @pl.when(jnp.logical_not(first & (to == 0)))
+            def _():
+                remote_in(a, to, me).start()
+
+    @pl.when(with_late)
+    def _():
+        pl.semaphore_wait(late_sem, 1)
+        for a in (K, V, Q, G):
+            remote_in(a, 0, me).start()
+
+    def wait_in(a, c):
+        src, dst, base = inputs[a]
         for d in range(2):
-            if isinstance(o, int):
-                if (o, d) == (0, 0):
-                    local_in(a).wait()
-                else:
-                    remote_in(a, me, device(o, d)).wait_recv()
-            else:
-                remote_in(a, me, device(o, d)).wait_recv()
+            head = c * 2 + d
+            pltpu.make_async_copy(
+                src.at[:, rows(me * ROWS, HEAD_DIM)], dst.at[rows(base + head * ROWS, ROWS)], recv_sem.at[a, head]
+            ).wait()
 
     def halo(i, buf):
         return pltpu.make_async_remote_copy(
@@ -118,10 +153,16 @@
         )
 
     for i, (a, buf) in enumerate(((K, kbuf), (V, vbuf))):
-        for o in range(8):
-            wait_in(a, o)
-
-        @pl.when(jnp.logical_not(last))
+        for c in range(CHUNKS):
+            wait_in(a, c)
+
+        if a == K:
+
+            @pl.when(has_next & jnp.logical_not(ends))
+            def _():
+                pl.semaphore_wait(next_sem, 1)
+
+        @pl.when(has_next)
         def _():
             halo(i, buf).start()
 
@@ -131,7 +172,7 @@
             def _(b):
                 kt[b] = kbuf[rows(b * CHUNK, CHUNK), :].T
 
-    @pl.when(jnp.logical_not(first))
+    @pl.when(has_prev)
     def _():
         halo(0, kbuf).wait_recv()
 
@@ -167,14 +208,13 @@
         for b in range(3):
             probs[c, b] = probs[c, b] * inverse
 
-    for o in range(8):
-        wait_in(Q, o)
-
     @pl.loop(0, CHUNKS)
-    def _(c):
+    def _(i):
+        c = (chip + i) % CHUNKS
+        wait_in(Q, c)
         softmax(c)
 
-    @pl.when(jnp.logical_not(first))
+    @pl.when(has_prev)
     def _():
         halo(1, vbuf).wait_recv()
 
@@ -230,15 +270,6 @@
             def _():
                 remote_out(a, to, me).start()
 
-    for o in range(8):
-        wait_in(G, o)
-
-    @pl.loop(0, CHUNKS)
-    def _(o):
-        c = partner_chip(o)
-        gradients(c)
-        send_out(DQ, c)
-
     def back(i, src, dst):
         return pltpu.make_async_remote_copy(
             src.at[pl.ds(CHUNKS * CHUNK, HALO * CHUNK)],
@@ -251,12 +282,23 @@
 
     tail = pl.ds(CHUNKS * CHUNK, HALO * CHUNK)
 
-    @pl.when(jnp.logical_not(first))
-    def _():
-        dk_out[tail, :] = (dk_acc[: HALO * CHUNK] * SCALE).astype(jnp.bfloat16)
-        dv_out[tail, :] = dv_acc[: HALO * CHUNK].astype(jnp.bfloat16)
-        back(0, dk_out, part_k).start()
-        back(1, dv_out, part_v).start()
+    @pl.when(has_prev & starts)
+    def _():
+        pl.semaphore_wait(prev_sem, 1)
+
+    @pl.loop(0, CHUNKS)
+    def _(i):
+        c = jnp.where(i < HALO, i, HALO + (chip + i) % (CHUNKS - HALO))
+        wait_in(G, c)
+        gradients(c)
+        send_out(DQ, c)
+
+        @pl.when(has_prev & (i == HALO - 1))
+        def _():
+            dv_out[tail, :] = dv_acc[: HALO * CHUNK].astype(jnp.bfloat16)
+            back(1, dv_out, part_v).start()
+            dk_out[tail, :] = (dk_acc[: HALO * CHUNK] * SCALE).astype(jnp.bfloat16)
+            back(0, dk_out, part_k).start()
 
     @pl.loop(0, 6)
     def _(i):
@@ -273,7 +315,7 @@
         part_k[...] = zero
         part_v[...] = zero
 
-    @pl.when(jnp.logical_not(last))
+    @pl.when(has_next)
     def _():
         back(0, dk_out, part_k).wait_recv()
         back(1, dv_out, part_v).wait_recv()
@@ -294,12 +336,12 @@
         for o, d in others:
             remote_in(a, device(o, d), me).wait_send()
 
-    @pl.when(jnp.logical_not(last))
+    @pl.when(has_next)
     def _():
         halo(0, kbuf).wait_send()
         halo(1, vbuf).wait_send()
 
-    @pl.when(jnp.logical_not(first))
+    @pl.when(has_prev)
     def _():
         back(0, dk_out, part_k).wait_send()
         back(1, dv_out, part_v).wait_send()
@@ -309,6 +351,14 @@
         for o, d in others:
             remote_out(a, device(o, d), me).wait_send()
             remote_out(a, me, device(o, d)).wait_recv()
+
+
+def store(a, b, c, x, y, z, sem):
+    copies = [pltpu.make_async_copy(src, dst, sem.at[i]) for i, (src, dst) in enumerate(((a, x), (b, y), (c, z)))]
+    for copy in copies:
+        copy.start()
+    for copy in copies:
+        copy.wait()
 
 
 def per_device(queries, key_vectors, value_vectors, grad_output):
@@ -317,7 +367,7 @@
     own, wide = CHUNKS * CHUNK, (CHUNKS + HALO) * CHUNK
     out = jax.ShapeDtypeStruct((tokens, width), bf16)
     anywhere = pl.BlockSpec(memory_space=pl.ANY)
-    return pl.pallas_call(
+    grads = pl.pallas_call(
         kernel,
         out_shape=(out, out, out),
         in_specs=[anywhere] * 4,
@@ -341,12 +391,24 @@
             pltpu.SemaphoreType.DMA((7, 16)),
             pltpu.SemaphoreType.DMA((4,)),
             pltpu.SemaphoreType.DMA((4,)),
+            pltpu.SemaphoreType.REGULAR,
+            pltpu.SemaphoreType.REGULAR,
+            pltpu.SemaphoreType.REGULAR,
         ],
         compiler_params=pltpu.CompilerParams(
-            collective_id=0, has_side_effects=True, vmem_limit_bytes=48 * 1024 * 1024
+            collective_id=0, has_side_effects=True, vmem_limit_bytes=52 * 1024 * 1024
         ),
         name="window_attention_backward",
     )(queries, key_vectors, value_vectors, grad_output)
+    return pl.pallas_call(
+        store,
+        out_shape=(out, out, out),
+        in_specs=[anywhere] * 3,
+        out_specs=(anywhere,) * 3,
+        scratch_shapes=[pltpu.SemaphoreType.DMA((3,))],
+        compiler_params=pltpu.CompilerParams(vmem_limit_bytes=8 * 1024 * 1024),
+        name="store",
+    )(*grads)
 
 
 def solution(mesh):

time: 73.4 us -> 66.9 us (0.911)
  local copies, waits for them, and re-layouts: 6.54 us -> 0 us
    unnamed x11 -> x0, local copies, waits for them, and re-layouts: 6.54 us -> none
    pallas_call x1, Pallas kernels: 65.9 us -> 64.1 us  [per_device(): pl.pallas_call(kernel, out_shape=(out, out, out), in_specs=[anywhere] * 4...]
    pallas_call x0 -> x1, Pallas kernels: none -> 1.17 us  [per_device(): pl.pallas_call(store, out_shape=(out, out, out), in_specs=[anywhere] * 3,...]
where the time goes in v2:
time: 66.9 us; the launch traced here: 65.9 us
  Pallas kernels  65.3 us (98%)
    pallas_call x1, Pallas kernels, per_device(): pl.pallas_call(kernel, out_shape=(out, out, out), in_specs=[anywhere] * 4...  64.1 us

profile of v2, /device:TPU:7, one launch (start us, length us, event | category | flops | bytes accessed | tf_op | source)
XLA Modules:
  0.0 65.9 jit_solution(7275891788761289731)
XLA Ops:
  0.6 64.1 %window_attention_backward.1 = (bf16[128,2048]{1,0:T(8,128)(2,1)S(1)}, bf16[128,2048]{1,0:T(8,128)(2,1)S(1)}, bf16[128,2048]{1,0:T(8,128)(2,1)S(1)}) custom-call(bf16[128,2048]{1,0:T(8,128)(2,1)} %q_hbm.1, bf16[128,2048]{1,0:T(8,128)(2,1)} %k_hbm.1, bf16[128,2048]{1,0:T(8,128)(2,1)} %v_hbm.1, bf16[128,2048]{1,0:T(8,128)(2,1)} %g_hbm.1), custom_call_target="tpu_custom_call" | custom-call | tf_op jit(solution)/shard_map/window_attention_backward/pallas_call | solution.py:370
  64.7 1.2 %store.1 = (bf16[128,2048]{1,0:T(8,128)(2,1)}, bf16[128,2048]{1,0:T(8,128)(2,1)}, bf16[128,2048]{1,0:T(8,128)(2,1)}) custom-call(bf16[128,2048]{1,0:T(8,128)(2,1)S(1)} %get-tuple-element.6.a, bf16[128,2048]{1,0:T(8,128)(2,1)S(1)} %get-tuple-element.7.b, bf16[128,2048]{1,0:T(8,128)(2,1)S(1)} %get-tuple-element.8.c), custom_call_target="tpu_custom_call" | custom-call | tf_op jit(solution)/shard_map/store/pallas_call | solution.py:403

commit v3 on v2

--- a/solution.py
+++ b/solution.py
@@ -12,6 +12,12 @@
 CHUNKS = 8
 HALO = 2
 RING = 16
+ORDER = (0, 5, 3, 7, 1, 4, 2, 6)
+EARLY = 3
+LATE_PLACE = 5
+RELAYS = (RING, RING, RING + 1, RING + 2)
+DIRECT = 2
+ORDER_HALO = (5, 3, 7, 1, 0, 4, 2, 6)
 ROWS = 128
 SCALE = HEAD_DIM ** (-0.5)
 LOG2E = 1.4426950408889634
@@ -26,7 +32,8 @@
     dq_hbm, dk_hbm, dv_hbm,
     kbuf, vbuf, qbuf, gbuf, kt, probs, dprobs,
     dk_acc, dv_acc, dq_out, dk_out, dv_out, part_k, part_v,
-    send_sem, recv_sem, hs_sem, hr_sem, late_sem, next_sem, prev_sem,
+    relay,
+    send_sem, recv_sem, hs_sem, hr_sem, turn_send, turn_recv, relay_send, relay_recv, late_sem, next_sem, prev_sem,
 ):
     s = lax.axis_index("seq")
     me = lax.axis_index("head")
@@ -39,7 +46,7 @@
     def partner_chip(o):
         return ((cx + o // 2) % 4) * 2 + (cy + o) % 2
 
-    others = [(o, d) for o in range(8) for d in range(2) if (o, d) != (0, 0)]
+    others = [(o, d) for o in ORDER for d in range(2) if (o, d) != (0, 0)]
 
     def device(o, d):
         return partner_chip(o) * 2 + (core + d) % 2
@@ -49,6 +56,11 @@
     starts = s % RING == 0
     ends = (s + 1) % RING == 0
     has_prev, has_next = jnp.logical_not(first), jnp.logical_not(last)
+    turn_to, turn_from = has_prev & starts, has_next & ends
+    relays, far_relay, slot = False, s == RING + 2, 0
+    for n in range(DIRECT, len(RELAYS)):
+        relays = relays | (s == RELAYS[n])
+        slot = jnp.where(s == RELAYS[n], n, slot)
 
     def signal(sem, block, head):
         pl.semaphore_signal(sem, inc=1, device_id=(block, head), device_id_type=MESH)
@@ -64,9 +76,14 @@
     def _():
         signal(barrier, s + 1, me)
 
-    @pl.when(has_prev & starts)
+    @pl.when(turn_to)
     def _():
         signal(barrier, s - 1, me)
+        signal(barrier, RING + 2, me)
+
+    @pl.when(relays)
+    def _():
+        signal(barrier, RING - 1, me)
 
     inputs = {K: (k_hbm, kbuf, HALO * CHUNK), V: (v_hbm, vbuf, HALO * CHUNK), Q: (q_hbm, qbuf, 0), G: (g_hbm, gbuf, 0)}
 
@@ -104,7 +121,7 @@
     dv_acc[...] = jnp.zeros_like(dv_acc)
 
     count = 15 - with_late.astype(jnp.int32) + jnp.logical_not(starts).astype(jnp.int32)
-    count = count + (has_next & ends).astype(jnp.int32)
+    count = count + turn_from.astype(jnp.int32) * (1 + len(RELAYS) - DIRECT) + far_relay.astype(jnp.int32)
     pl.semaphore_wait(barrier, count)
 
     @pl.when(late)
@@ -120,19 +137,24 @@
     def _():
         signal(prev_sem, s + 1, me)
 
-    for a in (K, V, Q, G):
+    for group in ((K,), (V,)):
         for o, d in others:
             to = device(o, d)
 
             @pl.when(jnp.logical_not(first & (to == 0)))
             def _():
-                remote_in(a, to, me).start()
+                for a in group:
+                    remote_in(a, to, me).start()
 
     @pl.when(with_late)
     def _():
         pl.semaphore_wait(late_sem, 1)
-        for a in (K, V, Q, G):
+        for a in (K, V):
             remote_in(a, 0, me).start()
+
+    for a in (Q, G):
+        for o, d in others:
+            remote_in(a, device(o, d), me).start()
 
     def wait_in(a, c):
         src, dst, base = inputs[a]
@@ -152,8 +174,39 @@
             device_id_type=MESH,
         )
 
+    def piece(i, n):
+        buf = (kbuf, vbuf)[i]
+        return pltpu.make_async_remote_copy(
+            buf.at[pl.ds(CHUNKS * CHUNK + n * ROWS, ROWS)],
+            buf.at[pl.ds(n * ROWS, ROWS)] if n < DIRECT else relay.at[i],
+            turn_send.at[i, n],
+            turn_recv.at[i, n] if n < DIRECT else relay_recv.at[i],
+            device_id=(RELAYS[n], me),
+            device_id_type=MESH,
+        )
+
+    def forward(i):
+        return pltpu.make_async_remote_copy(
+            relay.at[i],
+            (kbuf, vbuf)[i].at[rows(slot * ROWS, ROWS)],
+            relay_send.at[i],
+            turn_recv.at[i, slot],
+            device_id=(RING, me),
+            device_id_type=MESH,
+        )
+
+    def wait_piece(i, n):
+        buf = (kbuf, vbuf)[i]
+        pltpu.make_async_copy(
+            buf.at[pl.ds(CHUNKS * CHUNK, ROWS)], buf.at[pl.ds(n * ROWS, ROWS)], turn_recv.at[i, n]
+        ).wait()
+
+    def pass_on(i):
+        pltpu.make_async_copy(relay.at[i], relay.at[i], relay_recv.at[i]).wait()
+        forward(i).start()
+
     for i, (a, buf) in enumerate(((K, kbuf), (V, vbuf))):
-        for c in range(CHUNKS):
+        for c in range(CHUNKS - HALO, CHUNKS):
             wait_in(a, c)
 
         if a == K:
@@ -162,22 +215,23 @@
             def _():
                 pl.semaphore_wait(next_sem, 1)
 
-        @pl.when(has_next)
+        @pl.when(has_next & jnp.logical_not(ends))
         def _():
             halo(i, buf).start()
+
+        @pl.when(turn_from)
+        def _():
+            for n in range(len(RELAYS)):
+                piece(i, n).start()
+
+        for c in range(CHUNKS - HALO):
+            wait_in(a, c)
 
         if a == K:
 
             @pl.loop(HALO, HALO + CHUNKS)
             def _(b):
                 kt[b] = kbuf[rows(b * CHUNK, CHUNK), :].T
-
-    @pl.when(has_prev)
-    def _():
-        halo(0, kbuf).wait_recv()
-
-    for b in range(HALO):
-        kt[b] = kbuf[b * CHUNK : (b + 1) * CHUNK, :].T
 
     key_ids = lax.broadcasted_iota(jnp.int32, (CHUNK, CHUNK), 0)
     query_ids = lax.broadcasted_iota(jnp.int32, (CHUNK, CHUNK), 1)
@@ -208,16 +262,6 @@
         for b in range(3):
             probs[c, b] = probs[c, b] * inverse
 
-    @pl.loop(0, CHUNKS)
-    def _(i):
-        c = (chip + i) % CHUNKS
-        wait_in(Q, c)
-        softmax(c)
-
-    @pl.when(has_prev)
-    def _():
-        halo(1, vbuf).wait_recv()
-
     def gradients(c):
         queries = qbuf[rows(c * CHUNK, CHUNK), :]
         grads = gbuf[rows(c * CHUNK, CHUNK), :]
@@ -270,39 +314,25 @@
             def _():
                 remote_out(a, to, me).start()
 
-    def back(i, src, dst):
+    def back(i, part):
+        src, dst = ((dv_out, part_v), (dk_out, part_k))[i]
         return pltpu.make_async_remote_copy(
-            src.at[pl.ds(CHUNKS * CHUNK, HALO * CHUNK)],
-            dst,
-            hs_sem.at[2 + i],
-            hr_sem.at[2 + i],
+            src.at[pl.ds((CHUNKS + part) * CHUNK, CHUNK)],
+            dst.at[pl.ds(part * CHUNK, CHUNK)],
+            hs_sem.at[2 + 2 * part + i],
+            hr_sem.at[2 + 2 * part + i],
             device_id=(s - 1, me),
             device_id_type=MESH,
         )
 
-    tail = pl.ds(CHUNKS * CHUNK, HALO * CHUNK)
-
-    @pl.when(has_prev & starts)
-    def _():
-        pl.semaphore_wait(prev_sem, 1)
-
-    @pl.loop(0, CHUNKS)
-    def _(i):
-        c = jnp.where(i < HALO, i, HALO + (chip + i) % (CHUNKS - HALO))
-        wait_in(G, c)
-        gradients(c)
-        send_out(DQ, c)
-
-        @pl.when(has_prev & (i == HALO - 1))
-        def _():
-            dv_out[tail, :] = dv_acc[: HALO * CHUNK].astype(jnp.bfloat16)
-            back(1, dv_out, part_v).start()
-            dk_out[tail, :] = (dk_acc[: HALO * CHUNK] * SCALE).astype(jnp.bfloat16)
-            back(0, dk_out, part_k).start()
-
-    @pl.loop(0, 6)
-    def _(i):
-        c = (chip + i) % 6
+    def send_back(part):
+        src, dst = pl.ds(part * CHUNK, CHUNK), pl.ds((CHUNKS + part) * CHUNK, CHUNK)
+        dv_out[dst, :] = dv_acc[src, :].astype(jnp.bfloat16)
+        back(0, part).start()
+        dk_out[dst, :] = (dk_acc[src, :] * SCALE).astype(jnp.bfloat16)
+        back(1, part).start()
+
+    def finish(c):
         src = rows((c + HALO) * CHUNK, CHUNK)
         dst = rows(c * CHUNK, CHUNK)
         dv_out[dst, :] = dv_acc[src, :].astype(jnp.bfloat16)
@@ -310,41 +340,166 @@
         dk_out[dst, :] = (dk_acc[src, :] * SCALE).astype(jnp.bfloat16)
         send_out(DK, c)
 
-    @pl.when(last)
-    def _():
-        part_k[...] = zero
-        part_v[...] = zero
-
-    @pl.when(has_next)
-    def _():
-        back(0, dk_out, part_k).wait_recv()
-        back(1, dv_out, part_v).wait_recv()
-
-    @pl.loop(0, HALO)
-    def _(i):
-        p = (chip + i) % HALO
-        c = 6 + p
-        src = rows((c + HALO) * CHUNK, CHUNK)
-        dst = rows(c * CHUNK, CHUNK)
-        term = rows(p * CHUNK, CHUNK)
-        dv_out[dst, :] = (dv_acc[src, :] + part_v[term, :].astype(jnp.float32)).astype(jnp.bfloat16)
+    @pl.when(has_prev & starts)
+    def _():
+        pl.semaphore_wait(prev_sem, 1)
+
+    halo_chip = chip < HALO
+    base_order = []
+    for n in range(CHUNKS):
+        o = jnp.where(halo_chip, ORDER_HALO[n], ORDER[n])
+        base_order.append(((cx + 4 - o // 2) % 4) * 2 + (cy + o) % 2)
+
+    def moved(order, chunk, to, condition):
+        place = sum(jnp.where(order[n] == chunk, n, 0) for n in range(CHUNKS))
+        result = []
+        for n in range(CHUNKS):
+            after = order[min(n + 1, CHUNKS - 1)]
+            value = jnp.where((n >= place) & (n < to), after, jnp.where(n == to, chunk, order[n]))
+            result.append(jnp.where(condition & (place < to), value, order[n]))
+        return result
+
+    chunk_order = moved(base_order, 0, LATE_PLACE, first)
+    turn = turn_to
+    chunk_order = moved(chunk_order, 0, 5, turn)
+    chunk_order = moved(chunk_order, 1, 5, turn)
+
+    def chunk_at(i):
+        c = chunk_order[0]
+        for n in range(1, CHUNKS):
+            c = jnp.where(i == n, chunk_order[n], c)
+        return c
+
+    def wait_halo(a, buf):
+        @pl.when(has_prev & jnp.logical_not(starts))
+        def _():
+            halo(a, buf).wait_recv()
+
+        @pl.when(turn_to)
+        def _():
+            for n in range(len(RELAYS)):
+                wait_piece(a, n)
+
+    def weights(i, met):
+        c = chunk_at(i)
+
+        @pl.when(relays & (i == 1))
+        def _():
+            pass_on(0)
+
+        @pl.when((c < HALO) & (met == 0))
+        def _():
+            wait_halo(0, kbuf)
+
+            for b in range(HALO):
+                kt[b] = kbuf[b * CHUNK : (b + 1) * CHUNK, :].T
+
+        wait_in(Q, c)
+        softmax(c)
+        return met + (c < HALO).astype(jnp.int32)
+
+    lax.fori_loop(0, CHUNKS, weights, 0)
+
+    limit = EARLY
+
+    def step(i, carry):
+        done, sent, total = carry
+        c = chunk_at(i)
+
+        @pl.when(relays & (i == 2))
+        def _():
+            pass_on(1)
+
+        @pl.when((c < HALO) & (done % 4 == 0))
+        def _():
+            wait_halo(1, vbuf)
+
+        wait_in(G, c)
+        gradients(c)
+        send_out(DQ, c)
+        bit = 1
+        for n in range(1, CHUNKS):
+            bit = jnp.where(c == n, 2**n, bit)
+        done = done + bit
+
+        @pl.when(has_prev & (c == 0))
+        def _():
+            send_back(0)
+
+        @pl.when(has_prev & (c < HALO) & (done % 4 == 3))
+        def _():
+            send_back(1)
+
+        for b in range(3):
+            key = c - b
+            need = 0
+            for n in range(CHUNKS - HALO):
+                need = jnp.where((key == n) & ((done // 2**n) % 8 == 7) & (total < limit), 2**n, need)
+
+            @pl.when(need > 0)
+            def _():
+                finish(key)
+
+            sent = sent + need
+            total = total + (need > 0).astype(jnp.int32)
+
+        return done, sent, total
+
+    _, sent, _ = lax.fori_loop(0, CHUNKS, step, (0, 0, 0))
+
+    zero_part = jnp.zeros((CHUNK, HEAD_DIM), jnp.bfloat16)
+    for part in range(HALO):
+        window = pl.ds(part * CHUNK, CHUNK)
+
+        @pl.when(last)
+        def _():
+            part_k[window, :] = zero_part
+            part_v[window, :] = zero_part
+
+        @pl.when(has_next)
+        def _():
+            back(0, part).wait_recv()
+            back(1, part).wait_recv()
+
+        c = CHUNKS - HALO + part
+        src = pl.ds((c + HALO) * CHUNK, CHUNK)
+        dst = pl.ds(c * CHUNK, CHUNK)
+        dv_out[dst, :] = (dv_acc[src, :] + part_v[window, :].astype(jnp.float32)).astype(jnp.bfloat16)
         send_out(DV, c)
-        dk_out[dst, :] = (dk_acc[src, :] * SCALE + part_k[term, :].astype(jnp.float32)).astype(jnp.bfloat16)
+        dk_out[dst, :] = (dk_acc[src, :] * SCALE + part_k[window, :].astype(jnp.float32)).astype(jnp.bfloat16)
         send_out(DK, c)
+
+    for n in range(CHUNKS - HALO):
+
+        @pl.when((sent // 2**n) % 2 == 0)
+        def _():
+            finish(n)
 
     for a in (K, V, Q, G):
         for o, d in others:
             remote_in(a, device(o, d), me).wait_send()
 
-    @pl.when(has_next)
+    @pl.when(has_next & jnp.logical_not(ends))
     def _():
         halo(0, kbuf).wait_send()
         halo(1, vbuf).wait_send()
 
+    @pl.when(turn_from)
+    def _():
+        for n in range(len(RELAYS)):
+            piece(0, n).wait_send()
+            piece(1, n).wait_send()
+
+    @pl.when(relays)
+    def _():
+        forward(0).wait_send()
+        forward(1).wait_send()
+
     @pl.when(has_prev)
     def _():
-        back(0, dk_out, part_k).wait_send()
-        back(1, dv_out, part_v).wait_send()
+        for part in range(HALO):
+            back(0, part).wait_send()
+            back(1, part).wait_send()
 
     for a in (DQ, DK, DV):
         local_out(a).wait()
@@ -387,10 +542,15 @@
             pltpu.VMEM((wide, HEAD_DIM), bf16),
             pltpu.VMEM((HALO * CHUNK, HEAD_DIM), bf16),
             pltpu.VMEM((HALO * CHUNK, HEAD_DIM), bf16),
+            pltpu.VMEM((2, ROWS, HEAD_DIM), bf16),
             pltpu.SemaphoreType.DMA((7, 16)),
             pltpu.SemaphoreType.DMA((7, 16)),
-            pltpu.SemaphoreType.DMA((4,)),
-            pltpu.SemaphoreType.DMA((4,)),
+            pltpu.SemaphoreType.DMA((6,)),
+            pltpu.SemaphoreType.DMA((6,)),
+            pltpu.SemaphoreType.DMA((2, len(RELAYS))),
+            pltpu.SemaphoreType.DMA((2, len(RELAYS))),
+            pltpu.SemaphoreType.DMA((2,)),
+            pltpu.SemaphoreType.DMA((2,)),
             pltpu.SemaphoreType.REGULAR,
             pltpu.SemaphoreType.REGULAR,
             pltpu.SemaphoreType.REGULAR,

time: 66.9 us -> 62.7 us (0.937)
  the two profiles are of different devices: /device:TPU:7 before, /device:TPU:31 now
where the time goes in v3:
time: 62.7 us; the launch traced here: 62.6 us
  Pallas kernels  61.9 us (99%)
  between operations  0.64 us (1%)
    pallas_call x1, Pallas kernels, per_device(): pl.pallas_call(kernel, out_shape=(out, out, out), in_specs=[anywhere] * 4...  60.8 us

profile of v3, /device:TPU:31, one launch (start us, length us, event | category | flops | bytes accessed | tf_op | source)
XLA Modules:
  0.0 62.6 jit_solution(7460679397449887660)
XLA Ops:
  0.6 60.8 %window_attention_backward.1 = (bf16[128,2048]{1,0:T(8,128)(2,1)S(1)}, bf16[128,2048]{1,0:T(8,128)(2,1)S(1)}, bf16[128,2048]{1,0:T(8,128)(2,1)S(1)}) custom-call(bf16[128,2048]{1,0:T(8,128)(2,1)} %q_hbm.1, bf16[128,2048]{1,0:T(8,128)(2,1)} %k_hbm.1, bf16[128,2048]{1,0:T(8,128)(2,1)} %v_hbm.1, bf16[128,2048]{1,0:T(8,128)(2,1)} %g_hbm.1), custom_call_target="tpu_custom_call" | custom-call | tf_op jit(solution)/shard_map/window_attention_backward/pallas_call | solution.py:525
  61.4 1.2 %store.1 = (bf16[128,2048]{1,0:T(8,128)(2,1)}, bf16[128,2048]{1,0:T(8,128)(2,1)}, bf16[128,2048]{1,0:T(8,128)(2,1)}) custom-call(bf16[128,2048]{1,0:T(8,128)(2,1)S(1)} %get-tuple-element.6.a, bf16[128,2048]{1,0:T(8,128)(2,1)S(1)} %get-tuple-element.7.b, bf16[128,2048]{1,0:T(8,128)(2,1)S(1)} %get-tuple-element.8.c), custom_call_target="tpu_custom_call" | custom-call | tf_op jit(solution)/shard_map/store/pallas_call | solution.py:563
